TPU v7x, 512 devices: a whole 4x4x16 slice. The times are simulated.
512 devices in a mesh: seq: 128 (over x, z, core), head: 4 (over y).
Axes of the slice: x: 4, y: 4, z: 16, core: 2. Of those that a mesh axis runs over, the one named last changes fastest.
Arguments:
- tokens: bfloat16 [128, 128, 2048], P('seq'), may hold values from -6 to 6
- attn_gain: bfloat16 [2048], replicated, may hold values from 0.099609375 to 1.8984375
- q_gain: bfloat16 [64], replicated, may hold values from 0.099609375 to 1.8984375
- k_gain: bfloat16 [64], replicated, may hold values from 0.099609375 to 1.8984375
- ffn_gain: bfloat16 [2048], replicated, may hold values from 0.099609375 to 1.8984375
- w_query: bfloat16 [2048, 1280], P('seq', 'head'), may hold values from -0.125 to 0.125
- w_keyval: bfloat16 [2048, 640], P('seq'), may hold values from -0.125 to 0.125
- w_out: bfloat16 [1280, 2048], P('head', 'seq'), may hold values from -0.15625 to 0.15625
- prior_cache: bfloat16 [128, 512, 640], P(None, 'seq')
- prior_len: int32 [128], replicated, may hold values from 0 to 512, as said below
- stretch_len: int32 [128], replicated, may hold values from 1 to 128, as said below
Outputs:
- hidden: bfloat16 [128, 128, 2048], P('seq', 'head')
- ffn_input: bfloat16 [128, 128, 2048], P('seq', 'head')
- new_cache: bfloat16 [128, 128, 640], P('seq', 'head')
- decode_cache: bfloat16 [128, 512, 640], P('seq', 'head')
Inputs may be any that keep to these rules, and one draw needn't show every extreme that they name: `prior_len`: some request has all 512 slots in use. `stretch_len`: some request fills its stretch.
All inputs are finite; a program needn't handle non-finite values.
Results may differ from a plain program's by a relative error of at most 0.011.
The roundings to bfloat16 on the way count: a program that leaves them out, or rounds other values in their place, can miss the bound.
Values may be sent and summed in bfloat16 or wider, within the bound.
A program may use at most 64 MiB of HBM per device.

v0:
```python
import math
import jax
import jax.numpy as jnp
from jax import lax
from jax.sharding import PartitionSpec as P

HD = 64
QH = 20
KVH = 5
epsilon = 1e-06


def rms_norm(values, gain):
    return values * lax.rsqrt(jnp.mean(values * values, axis=-1, keepdims=True) + epsilon) * gain


def rotary(values, positions):
    middle = values.shape[-1] // 2
    inverse = jnp.exp(
        jnp.arange(middle, dtype=jnp.float32) * (-2.0 * math.log(10000.0) / values.shape[-1])
    )
    angles = positions.astype(jnp.float32)[:, None] * inverse[None, :]
    cosine = jnp.concatenate([jnp.cos(angles), jnp.cos(angles)], axis=-1)[:, None, :]
    sine = jnp.concatenate([jnp.sin(angles), jnp.sin(angles)], axis=-1)[:, None, :]
    turned = jnp.concatenate([-values[..., middle:], values[..., :middle]], axis=-1)
    return values * cosine + turned * sine


def attend_dense(
    query, prior_keys, prior_values, fresh_keys, fresh_values, prior_count, score_scale
):
    length = fresh_keys.shape[0]
    stored = prior_keys.shape[0]
    all_keys = jnp.concatenate([prior_keys, fresh_keys], axis=0)
    all_values = jnp.concatenate([prior_values, fresh_values], axis=0)
    scores = (
        jnp.einsum("qhd,khd->hqk", query, all_keys, preferred_element_type=jnp.float32)
        * score_scale
    )
    offsets = jnp.arange(length, dtype=jnp.int32)
    earlier = jnp.arange(stored, dtype=jnp.int32)[None, :] < prior_count
    allowed = jnp.concatenate(
        [jnp.broadcast_to(earlier, (length, stored)), offsets[None, :] <= offsets[:, None]], axis=1
    )
    scores = jnp.where(allowed[None], scores, -jnp.inf)
    top = jnp.max(scores, axis=-1, keepdims=True)
    weights = jnp.exp(scores - top)
    total = jnp.sum(weights, axis=-1)
    mixed = jnp.einsum(
        "hqk,khd->qhd", weights.astype(jnp.bfloat16), all_values, preferred_element_type=jnp.float32
    )
    return mixed / total.T[:, :, None]


def shards(
    tokens,
    attn_gain,
    q_gain,
    k_gain,
    ffn_gain,
    w_query,
    w_keyval,
    w_out,
    prior_cache,
    prior_len,
    stretch_len,
):
    seq_index = lax.axis_index("seq")
    head_index = lax.axis_index("head")
    head_count = lax.axis_size("head")
    local_requests, length, width = tokens.shape
    token_count = local_requests * length
    width_kv = KVH * HD
    local_heads = QH // head_count
    score_scale = 1.0 / math.sqrt(HD)
    flat = tokens.reshape(token_count, width)
    normed = rms_norm(flat.astype(jnp.float32), attn_gain.astype(jnp.float32)).astype(jnp.bfloat16)
    first = jnp.dot(
        normed,
        lax.all_gather(w_query, "seq", axis=0, tiled=True),
        preferred_element_type=jnp.float32,
    )
    second = jnp.dot(
        normed,
        lax.all_gather(w_keyval, "seq", axis=0, tiled=True),
        preferred_element_type=jnp.float32,
    )
    query = first
    prior_counts = lax.dynamic_slice_in_dim(prior_len, seq_index * local_requests, local_requests)
    stretch_counts = lax.dynamic_slice_in_dim(
        stretch_len, seq_index * local_requests, local_requests
    )
    offsets = jnp.arange(length, dtype=jnp.int32)
    positions = (prior_counts[:, None] + offsets[None, :]).reshape(token_count)
    query = rotary(
        rms_norm(query.reshape(token_count, local_heads, HD), q_gain.astype(jnp.float32)), positions
    ).astype(jnp.bfloat16)
    fresh_keys = rotary(
        rms_norm(second[:, :width_kv].reshape(token_count, KVH, HD), k_gain.astype(jnp.float32)),
        positions,
    ).astype(jnp.bfloat16)
    fresh_values = second[:, width_kv:].reshape(token_count, KVH, HD).astype(jnp.bfloat16)
    gathered_cache = lax.all_to_all(prior_cache, "seq", split_axis=0, concat_axis=1, tiled=True)
    stored = gathered_cache.shape[1]
    block_slots = stored // head_count
    decode_cache = lax.dynamic_slice_in_dim(
        gathered_cache, head_index * block_slots, block_slots, 1
    )
    group = (head_index * local_heads + jnp.arange(local_heads, dtype=jnp.int32)) // (QH // KVH)
    prior_keys = jnp.take(
        gathered_cache[:, :, :width_kv].reshape(local_requests, stored, KVH, HD), group, axis=2
    )
    prior_values = jnp.take(
        gathered_cache[:, :, width_kv:].reshape(local_requests, stored, KVH, HD), group, axis=2
    )
    stretch_keys = jnp.take(fresh_keys.reshape(local_requests, length, KVH, HD), group, axis=2)
    stretch_values = jnp.take(fresh_values.reshape(local_requests, length, KVH, HD), group, axis=2)
    query_blocks = query.reshape(local_requests, length, local_heads, HD)
    mixed = attend_dense(
        query_blocks[0],
        prior_keys[0],
        prior_values[0],
        stretch_keys[0],
        stretch_values[0],
        prior_counts[0],
        score_scale,
    )
    results = mixed.astype(jnp.bfloat16).reshape(length, local_heads * HD)
    terms = jnp.dot(
        results,
        lax.all_gather(w_out, "seq", axis=1, tiled=True),
        preferred_element_type=jnp.float32,
    )
    share_rows = length // head_count
    summed = lax.psum_scatter(
        terms.reshape(local_requests, length, width).astype(jnp.bfloat16),
        "head",
        scatter_dimension=1,
        tiled=True,
    ).astype(jnp.float32)
    own_tokens = lax.dynamic_slice_in_dim(tokens, head_index * share_rows, share_rows, 1).astype(
        jnp.float32
    )
    residual = own_tokens + summed
    row_offsets = head_index * share_rows + jnp.arange(share_rows, dtype=jnp.int32)
    valid = row_offsets[None, :] < stretch_counts[:, None]
    hidden = jnp.where(valid[:, :, None], residual, 0.0).astype(jnp.bfloat16)
    ffn_input = jnp.where(
        valid[:, :, None], rms_norm(residual, ffn_gain.astype(jnp.float32)), 0.0
    ).astype(jnp.bfloat16)
    fresh = jnp.concatenate(
        [
            fresh_keys.reshape(local_requests, length, width_kv),
            fresh_values.reshape(local_requests, length, width_kv),
        ],
        axis=2,
    )
    fresh = lax.dynamic_slice_in_dim(fresh, head_index * share_rows, share_rows, 1)
    fresh = jnp.where(valid[:, :, None], fresh, jnp.zeros_like(fresh))
    return (hidden, ffn_input, fresh, decode_cache)


def solution(mesh):
    placed = (
        P("seq", None, None),
        P(),
        P(),
        P(),
        P(),
        P("seq", "head"),
        P("seq", None),
        P("head", "seq"),
        P(None, "seq", None),
        P(),
        P(),
    )
    return jax.shard_map(
        shards,
        mesh=mesh,
        in_specs=placed,
        out_specs=(
            P("seq", "head", None),
            P("seq", "head", None),
            P("seq", "head", None),
            P("seq", "head", None),
        ),
        check_vma=False,
    )
```

profile of v0, /device:TPU:2, one launch (start us, length us, event | category | flops | bytes accessed | tf_op | source)
XLA Modules:
  0.0 474.5 jit_solution(8410260316562523940)
XLA Ops:
  7.2 0.7 all-gather.6.cloned.1.call-update
  8.0 0.7 all-gather.4.cloned.1.call-update
  8.7 19.5 %all-to-all-start = ((bf16[128,4,640]{2,1,0:T(4,128)(2,1)}), bf16[128,4,640]{2,1,0:T(4,128)(2,1)S(1)}, u32[]{:S(2)}, u32[]{:S(2)}) async-start(bf16[128,4,640]{2,1,0:T(4,128)(2,1)} %param.23), calls=%async_computation | async-start | bytes 1310720 | tf_op jit(solution)/shard_map/all_to_all | solution.py:103
  28.2 0.7 all-gather.8.cloned.1.call-update
  29.0 0.7 convert_element_type.100
  29.7 0.7 convert_element_type.110
  30.3 0.7 convert_element_type.107
  31.0 1.2 dynamic_slice.17
  32.2 0.6 iota_compare_fusion.1
  33.0 0.7 add_convert_fusion
  34.1 33.9 %all-to-all-done = bf16[128,4,640]{2,1,0:T(4,128)(2,1)S(1)} async-done(((bf16[128,4,640]{2,1,0:T(4,128)(2,1)}), bf16[128,4,640]{2,1,0:T(4,128)(2,1)S(1)}, u32[]{:S(2)}, u32[]{:S(2)}) %all-to-all-start) | async-done | bytes 655392 | tf_op jit(solution)/shard_map/all_to_all | solution.py:103
  68.3 87.2 %all-gather.6.cloned.1.call-done = bf16[2048,320]{1,0:T(8,128)(2,1)} async-done(((bf16[16,320]{1,0:T(8,128)(2,1)}), bf16[2048,320]{1,0:T(8,128)(2,1)}) %all-gather.6.cloned.1.call-update) | async-done | bytes 1310736 | tf_op jit(solution)/shard_map/all_gather | solution.py:80
  155.5 1.7 copy.41
  159.5 136.3 %all-gather.4.cloned.1.call-done = bf16[2048,640]{1,0:T(8,128)(2,1)} async-done(((bf16[16,640]{1,0:T(8,128)(2,1)}), bf16[2048,640]{1,0:T(8,128)(2,1)}) %all-gather.4.cloned.1.call-update) | async-done | bytes 2621456 | tf_op jit(solution)/shard_map/all_gather | solution.py:85
  295.8 2.9 fusion.17
  301.8 133.8 %all-gather.8.cloned.1.call-done = bf16[320,2048]{0,1:T(8,128)(2,1)} async-done(((bf16[320,16]{0,1:T(8,128)(2,1)}), bf16[320,2048]{0,1:T(8,128)(2,1)}) %all-gather.8.cloned.1.call-update) | async-done | bytes 1310736 | tf_op jit(solution)/shard_map/all_gather | solution.py:131
  435.6 2.8 fusion
  438.5 0.6 dynamic_slice.15
  439.2 0.7 add_compare_fusion
  439.8 0.7 constant_dynamic-slice_fusion
  440.8 0.7 copy.44
  441.5 23.6 %reduce-scatter.2.cloned.1.call-done = bf16[1,32,2048]{2,1,0:T(8,128)(2,1)} async-done(((bf16[1,128,2048]{2,1,0:T(8,128)(2,1)}), bf16[1,32,2048]{2,1,0:T(8,128)(2,1)}) %reduce-scatter.2.cloned.1.call-update) | async-done | bytes 131088 | tf_op jit(solution)/shard_map/reduce_scatter | solution.py:135
  465.2 1.1 multiply_reduce_fusion
  466.2 1.7 select_convert_fusion
  (56 shorter events, 6.6 us)
Async XLA Ops:
  7.2 26.7 %copy-start = (bf16[1,128,2048]{2,1,0:T(8,128)(2,1)S(1)}, bf16[1,128,2048]{2,1,0:T(8,128)(2,1)}, u32[]{:S(2)}) copy-start(bf16[1,128,2048]{2,1,0:T(8,128)(2,1)} %param.15) | copy-start | bytes 1572868
  7.2 148.3 %all-gather.6.cloned.1.call-start = ((), (), s32[]{:S(2)}) async-start(), calls=%async_computation.3 | async-start | bytes 1585152 | tf_op jit(solution)/shard_map/all_gather | solution.py:80
  7.9 287.9 %all-gather.4.cloned.1.call-start = ((), (), s32[]{:S(2)}) async-start(), calls=%async_computation.2 | async-start | bytes 2641920 | tf_op jit(solution)/shard_map/all_gather | solution.py:85
  8.7 59.3 %all-to-all-start = ((bf16[128,4,640]{2,1,0:T(4,128)(2,1)}), bf16[128,4,640]{2,1,0:T(4,128)(2,1)S(1)}, u32[]{:S(2)}, u32[]{:S(2)}) async-start(bf16[128,4,640]{2,1,0:T(4,128)(2,1)} %param.23), calls=%async_computation | async-start | bytes 1310720 | tf_op jit(solution)/shard_map/all_to_all | solution.py:103
  28.2 407.4 %all-gather.8.cloned.1.call-start = ((), (), s32[]{:S(2)}) async-start(), calls=%async_computation.4 | async-start | bytes 1585152 | tf_op jit(solution)/shard_map/all_gather | solution.py:131
  28.9 436.2 %reduce-scatter.2.cloned.1.call-start = ((), (), s32[]{:S(2)}) async-start(), calls=%async_computation.5 | async-start | bytes 655360 | tf_op jit(solution)/shard_map/reduce_scatter | solution.py:135
  301.8 136.7 %copy-start.1 = (bf16[2048]{0:T(1024)(128)(2,1)S(1)}, bf16[2048]{0:T(1024)(128)(2,1)}, u32[]{:S(2)}) copy-start(bf16[2048]{0:T(1024)(128)(2,1)} %param.19) | copy-start | bytes 12292
  301.8 136.7 %copy-start.3 = (s32[128]{0:T(128)S(1)}, s32[128]{0:T(128)}, u32[]{:S(2)}) copy-start(s32[128]{0:T(128)} %param.25) | copy-start | bytes 1540
  301.8 137.3 %copy-start.2 = (bf16[64]{0:T(256)(128)(2,1)S(1)}, bf16[64]{0:T(256)(128)(2,1)}, u32[]{:S(2)}) copy-start(bf16[64]{0:T(256)(128)(2,1)} %param.18) | copy-start | bytes 388
Sparse Core Ops, SparseCore 0:
  11.0 144.3 all-gather.5
  158.5 137.2 all-gather.3
  298.8 136.6 all-gather.7
  438.6 26.5 reduce-scatter.1
where the time goes:
time: 475 us; the launch traced here: 474 us
  waiting for transfers between devices  417 us (88%)
  starting transfers between devices  19.7 us (4%)
  between operations  14.1 us (3%)
  other arithmetic  8.47 us (2%)
  local copies, waits for them, and re-layouts  8.03 us (2%)
  matrix products  7.37 us (2%)
    all_gather x1, waiting for transfers between devices, shards(): lax.all_gather(w_keyval, 'seq', axis=0, tiled=True)  136 us
    all_gather x1, waiting for transfers between devices, shards(): lax.all_gather(w_out, 'seq', axis=1, tiled=True)  134 us
    all_gather x1, waiting for transfers between devices, shards(): lax.all_gather(w_query, 'seq', axis=0, tiled=True)  87.2 us
    all_to_all x1, waiting for transfers between devices, shards(): lax.all_to_all(prior_cache, 'seq', split_axis=0, concat_axis=1, tiled=True)  33.9 us
    reduce_scatter x1, waiting for transfers between devices, shards(): lax.psum_scatter(terms.reshape(local_requests, length, width).astype(jnp....  23.6 us
    all_to_all x1, starting transfers between devices, shards(): lax.all_to_all(prior_cache, 'seq', split_axis=0, concat_axis=1, tiled=True)  19.5 us
  transfers between devices with their start and end apart: 5, of which 5 were waited for; matrix products, arithmetic and copies ran while one was open for 4% of the time, Pallas kernels for 0%

commit v1 on v0

--- a/solution.py
+++ b/solution.py
@@ -128,7 +128,9 @@
     results = mixed.astype(jnp.bfloat16).reshape(length, local_heads * HD)
     terms = jnp.dot(
         results,
-        lax.all_gather(w_out, "seq", axis=1, tiled=True),
+        jnp.concatenate(
+            lax.all_to_all(jnp.stack([w_out] * lax.axis_size("seq")), "seq", 0, 0), axis=1
+        ),
         preferred_element_type=jnp.float32,
     )
     share_rows = length // head_count

time: 475 us -> 350 us (0.74)
  waiting for transfers between devices: 417 us -> 275 us
  starting transfers between devices: 19.7 us -> 26.6 us
  local copies, waits for them, and re-layouts: 8.03 us -> 13.5 us
    all_gather x1 -> x0, waiting for transfers between devices: 134 us -> none  [shards(): lax.all_gather(w_out, 'seq', axis=1, tiled=True)]
    all_to_all x0 -> x1, starting transfers between devices: none -> 6.95 us  [shards(): lax.all_to_all(jnp.stack([w_out] * lax.axis_size('seq')), 'seq', 0, 0)]
    all_gather x1, waiting for transfers between devices: 136 us -> 131 us  [shards(): lax.all_gather(w_keyval, 'seq', axis=0, tiled=True)]
  transfers between devices with their start and end apart: 5 -> 5, of which waited for: 5 -> 4; matrix products, arithmetic and copies ran while one was open for 4% -> 8% of each run, Pallas kernels for 0% -> 0%
where the time goes in v1:
time: 350 us; the launch traced here: 349 us
  waiting for transfers between devices  275 us (79%)
  starting transfers between devices  26.6 us (8%)
  between operations  14.2 us (4%)
  local copies, waits for them, and re-layouts  13.5 us (4%)
  other arithmetic  11.2 us (3%)
  matrix products  8.7 us (2%)
    all_gather x1, waiting for transfers between devices, shards(): lax.all_gather(w_keyval, 'seq', axis=0, tiled=True)  131 us
    all_gather x1, waiting for transfers between devices, shards(): lax.all_gather(w_query, 'seq', axis=0, tiled=True)  82.6 us
    all_to_all x1, waiting for transfers between devices, shards(): lax.all_to_all(prior_cache, 'seq', split_axis=0, concat_axis=1, tiled=True)  37.7 us
    reduce_scatter x1, waiting for transfers between devices, shards(): lax.psum_scatter(terms.reshape(local_requests, length, width).astype(jnp....  22.9 us
    all_to_all x1, starting transfers between devices, shards(): lax.all_to_all(prior_cache, 'seq', split_axis=0, concat_axis=1, tiled=True)  19.5 us
  transfers between devices with their start and end apart: 5, of which 4 were waited for; matrix products, arithmetic and copies ran while one was open for 8% of the time, Pallas kernels for 0%

profile of v1, /device:TPU:2, one launch (start us, length us, event | category | flops | bytes accessed | tf_op | source)
XLA Modules:
  0.0 349.4 jit_solution(8276663672337080145)
XLA Ops:
  7.9 19.5 %all-to-all-start = ((bf16[128,4,640]{2,1,0:T(4,128)(2,1)}), bf16[128,4,640]{2,1,0:T(4,128)(2,1)S(1)}, u32[]{:S(2)}, u32[]{:S(2)}) async-start(bf16[128,4,640]{2,1,0:T(4,128)(2,1)} %param.23), calls=%async_computation | async-start | bytes 1310720 | tf_op jit(solution)/shard_map/all_to_all | solution.py:103
  27.5 0.7 all-gather.3.cloned.1.call-update
  28.2 1.2 dynamic_slice.17
  29.5 37.7 %all-to-all-done = bf16[128,4,640]{2,1,0:T(4,128)(2,1)S(1)} async-done(((bf16[128,4,640]{2,1,0:T(4,128)(2,1)}), bf16[128,4,640]{2,1,0:T(4,128)(2,1)S(1)}, u32[]{:S(2)}, u32[]{:S(2)}) %all-to-all-start) | async-done | bytes 655392 | tf_op jit(solution)/shard_map/all_to_all | solution.py:103
  67.2 2.0 stack.2
  69.2 7.0 %all-to-all-start.1 = ((bf16[128,320,16]{1,2,0:T(8,128)(2,1)}), bf16[128,320,16]{1,2,0:T(8,128)(2,1)S(1)}, u32[]{:S(2)}, u32[]{:S(2)}) async-start(bf16[128,320,16]{1,2,0:T(8,128)(2,1)} %stack.2), calls=%async_computation.1 | async-start | bytes 3145728 | tf_op jit(solution)/shard_map/all_to_all | solution.py:132
  78.7 82.6 %all-gather.5.cloned.1.call-done = bf16[2048,320]{1,0:T(8,128)(2,1)} async-done(((bf16[16,320]{1,0:T(8,128)(2,1)}), bf16[2048,320]{1,0:T(8,128)(2,1)}) %all-gather.5.cloned.1.call-update) | async-done | bytes 1310736 | tf_op jit(solution)/shard_map/all_gather | solution.py:80
  161.3 2.6 copy.42
  164.0 0.9 fusion.48
  165.1 1.1 copy.43
  167.5 2.1 multiply_reduce_fusion.2
  171.0 1.0 fusion.30
  172.0 130.7 %all-gather.3.cloned.1.call-done = bf16[2048,640]{1,0:T(8,128)(2,1)} async-done(((bf16[16,640]{1,0:T(8,128)(2,1)}), bf16[2048,640]{1,0:T(8,128)(2,1)}) %all-gather.3.cloned.1.call-update) | async-done | bytes 2621456 | tf_op jit(solution)/shard_map/all_gather | solution.py:85
  302.7 2.9 fusion.17
  306.4 0.7 slice_negate_fusion
  308.5 0.7 fusion.41
  309.2 1.7 fusion.49
  312.0 1.5 fusion
  314.9 0.7 constant_dynamic-slice_fusion
  315.6 0.8 fusion.36
  316.5 0.7 copy.45
  317.2 22.9 %reduce-scatter.2.cloned.1.call-done = bf16[1,32,2048]{2,1,0:T(8,128)(2,1)} async-done(((bf16[1,128,2048]{2,1,0:T(8,128)(2,1)}), bf16[1,32,2048]{2,1,0:T(8,128)(2,1)}) %reduce-scatter.2.cloned.1.call-update) | async-done | bytes 131088 | tf_op jit(solution)/shard_map/reduce_scatter | solution.py:137
  340.1 1.1 multiply_reduce_fusion
  341.2 1.7 select_convert_fusion
  (80 shorter events, 10.7 us)
Async XLA Ops:
  7.2 154.2 %all-gather.5.cloned.1.call-start = ((), (), s32[]{:S(2)}) async-start(), calls=%async_computation.4 | async-start | bytes 1585152 | tf_op jit(solution)/shard_map/all_gather | solution.py:80
  7.9 59.3 %all-to-all-start = ((bf16[128,4,640]{2,1,0:T(4,128)(2,1)}), bf16[128,4,640]{2,1,0:T(4,128)(2,1)S(1)}, u32[]{:S(2)}, u32[]{:S(2)}) async-start(bf16[128,4,640]{2,1,0:T(4,128)(2,1)} %param.23), calls=%async_computation | async-start | bytes 1310720 | tf_op jit(solution)/shard_map/all_to_all | solution.py:103
  27.4 275.3 %all-gather.3.cloned.1.call-start = ((), (), s32[]{:S(2)}) async-start(), calls=%async_computation.3 | async-start | bytes 2641920 | tf_op jit(solution)/shard_map/all_gather | solution.py:85
  29.5 141.6 %copy-start.10 = (pred[5]{0:T(512)(128)(4,1)}, pred[5]{0:T(512)(128)(4,1)S(1)}, u32[]{:S(2)}) copy-start(pred[5]{0:T(512)(128)(4,1)S(1)} %compare_and_fusion) | copy-start | bytes 19
  69.2 7.7 %copy-start.12 = (bf16[64]{0:T(256)(128)(2,1)S(1)}, bf16[64]{0:T(256)(128)(2,1)}, u32[]{:S(2)}) copy-start(bf16[64]{0:T(256)(128)(2,1)} %param.18) | copy-start | bytes 388
  69.2 7.7 %copy-start.14 = (bf16[64]{0:T(256)(128)(2,1)S(1)}, bf16[64]{0:T(256)(128)(2,1)}, u32[]{:S(2)}) copy-start(bf16[64]{0:T(256)(128)(2,1)} %param.17) | copy-start | bytes 388
  69.2 7.7 %copy-start.8 = (bf16[2048]{0:T(1024)(128)(2,1)S(1)}, bf16[2048]{0:T(1024)(128)(2,1)}, u32[]{:S(2)}) copy-start(bf16[2048]{0:T(1024)(128)(2,1)} %param.16) | copy-start | bytes 12292
  69.2 8.6 %copy-start = (bf16[1,128,2048]{2,1,0:T(8,128)(2,1)S(1)}, bf16[1,128,2048]{2,1,0:T(8,128)(2,1)}, u32[]{:S(2)}) copy-start(bf16[1,128,2048]{2,1,0:T(8,128)(2,1)} %param.15) | copy-start | bytes 1572868
  69.2 242.8 %all-to-all-start.1 = ((bf16[128,320,16]{1,2,0:T(8,128)(2,1)}), bf16[128,320,16]{1,2,0:T(8,128)(2,1)S(1)}, u32[]{:S(2)}, u32[]{:S(2)}) async-start(bf16[128,320,16]{1,2,0:T(8,128)(2,1)} %stack.2), calls=%async_computation.1 | async-start | bytes 3145728 | tf_op jit(solution)/shard_map/all_to_all | solution.py:132
  76.1 264.0 %reduce-scatter.2.cloned.1.call-start = ((), (), s32[]{:S(2)}) async-start(), calls=%async_computation.5 | async-start | bytes 655360 | tf_op jit(solution)/shard_map/reduce_scatter | solution.py:137
  76.9 229.4 %copy-start.11 = (f32[64]{0:T(128)}, f32[64]{0:T(128)S(1)}, u32[]{:S(2)}) copy-start(f32[64]{0:T(128)S(1)} %convert_element_type.110) | copy-start | bytes 772
  77.6 228.0 %copy-start.7 = (s32[1024]{0:T(1024)}, s32[1024]{0:T(1024)S(1)}, u32[]{:S(2)}) copy-start(s32[1024]{0:T(1024)S(1)} %pad_clamp_fusion) | copy-start | bytes 12292
  167.4 135.3 %copy-start.1 = (bf16[1,128,2048]{2,1,0:T(8,128)(2,1)S(1)}, bf16[1,128,2048]{2,1,0:T(8,128)(2,1)}, u32[]{:S(2)}) copy-start(bf16[1,128,2048]{2,1,0:T(8,128)(2,1)} %param.15) | copy-start | bytes 1572868
  169.7 0.7 copy-start.2
  306.3 0.8 copy-start.6
  309.2 2.2 copy-start.3
  312.0 1.6 copy-start.15
  312.0 2.1 copy-start.13
  312.0 2.2 copy-start.9
  312.0 3.6 %copy-start.4 = (f32[128,5,32]{0,2,1:T(8,128)S(1)}, f32[128,5,32]{0,2,1:T(8,128)}, u32[]{:S(2)}) copy-start(f32[128,5,32]{0,2,1:T(8,128)} %get-tuple-element.18) | copy-start | bytes 245764
  312.0 3.6 %copy-start.5 = (f32[128,5,32]{0,2,1:T(8,128)S(1)}, f32[128,5,32]{0,2,1:T(8,128)}, u32[]{:S(2)}) copy-start(f32[128,5,32]{0,2,1:T(8,128)} %get-tuple-element.21) | copy-start | bytes 245764
Sparse Core Ops, SparseCore 0:
  11.0 150.2 all-gather.4
  164.4 138.2 all-gather.2
  313.6 26.4 reduce-scatter.1
